TPU v7x, 256 devices: a whole 4x4x8 slice. The times are simulated.
256 devices in a mesh: row: 32 (over x_hi, z, core), col: 8 (over x_lo, y).
Axes of the slice: x: 4 (x_hi: 2, x_lo: 2; x = x_hi * 2 + x_lo), y: 4, z: 8, core: 2. Of those that a mesh axis runs over, the one named last changes fastest.
Arguments:
- amplitudes: float32 [1024, 64, 1200], P('col', 'row'), may hold values from -6 to 6
- integrals: float32 [64, 1200, 8, 1200], P('row', None, 'col'), may hold values from -0.09375 to 0.09375
- pair_energy: float32 [1024], P(('row', 'col')), may hold values from -4 to -1
- block_energy: float32 [8], replicated, may hold values from 0.2 to 3
- virtual_energy: float32 [1200], replicated, may hold values from 0.2 to 3
Outputs:
- new_amplitudes: float32 [1024, 8, 1200], P(('row', 'col'))
All inputs are finite; a program needn't handle non-finite values.
Results may differ from a plain program's by a relative error of at most 0.00027.
Values sent between devices are 32-bit elements; how exact they have to be, the bound alone decides.
A program may use at most 128 MiB of HBM per device.

v0:
```python
import jax
import jax.numpy as jnp
from jax import lax
from jax.sharding import PartitionSpec as P


def per_device(amplitudes, integrals, pair_energy, block_energy, virtual_energy):
    row_size = lax.axis_size("row")
    gathered = lax.all_gather(amplitudes, "col", axis=0, tiled=True)
    pair_count = gathered.shape[0]
    contract_len = gathered.shape[1] * gathered.shape[2]
    flattened = gathered.reshape(pair_count, contract_len)
    a_local = integrals.shape[2]
    virt_width = integrals.shape[3]
    weights = integrals.reshape(contract_len, a_local * virt_width)
    row_block = pair_count // row_size
    summed = lax.psum_scatter(
        jnp.dot(
            flattened, weights, precision=lax.Precision.HIGHEST, preferred_element_type=jnp.float32
        ),
        "row",
        scatter_dimension=0,
        tiled=True,
    )
    reshaped = summed.reshape(row_block, a_local, virt_width)
    arrived = lax.all_to_all(reshaped, "col", split_axis=0, concat_axis=1, tiled=True)
    denominator = (
        pair_energy[:, None, None] - block_energy[None, :, None] - virtual_energy[None, None, :]
    )
    return arrived / denominator


def solution(mesh):
    placed = (P("col", "row", None), P("row", None, "col", None), P(("row", "col")), P(), P())
    return jax.shard_map(
        per_device,
        mesh=mesh,
        in_specs=placed,
        out_specs=P(("row", "col"), None, None),
        check_vma=False,
    )
```

profile of v0, /device:TPU:4, one launch (start us, length us, event | category | flops | bytes accessed | tf_op | source)
XLA Modules:
  0.0 327.4 jit_solution(6195841070064501322)
XLA Ops:
  6.5 0.0 all-gather.2.cloned.1.call-start
  6.5 0.7 all-gather.2.cloned.1.call-update
  7.3 0.0 reduce-scatter.2.cloned.1.call-start
  7.3 9.8 %copy.10 = f32[2,1200,1,1200]{3,1,2,0:T(8,128)} copy(f32[2,1200,1,1200]{3,2,1,0:T(1,128)} %param.6) | data formatting | bytes 23040000
  17.1 109.0 %all-gather.2.cloned.1.call-done = f32[1024,2,1200]{0,2,1:T(8,128)} async-done(((f32[128,2,1200]{0,2,1:T(8,128)}), f32[1024,2,1200]{0,2,1:T(8,128)}) %all-gather.2.cloned.1.call-update) | async-done | bytes 9830416 | tf_op jit(solution)/shard_map/all_gather | solution.py:9
  126.1 0.0 copy-start.1
  126.1 0.0 copy-start.2
  126.1 0.0 copy-start
  126.1 47.6 %fusion = f32[1024,1200]{1,0:T(8,128)} fusion(f32[1024,2400]{0,1:T(8,128)} %bitcast.13, f32[2400,1200]{1,0:T(8,128)} %bitcast.10), kind=kOutput, calls=%fused_computation.2 | convolution fusion | flops 35389440000 | bytes 26265600 | tf_op jit(solution)/shard_map/dot_general | solution.py:18
  173.7 0.0 reduce-scatter.2.cloned.1.call-update
  173.7 132.8 %reduce-scatter.2.cloned.1.call-done = f32[32,1200]{1,0:T(8,128)} async-done(((f32[1024,1200]{1,0:T(8,128)}), f32[32,1200]{1,0:T(8,128)}) %reduce-scatter.2.cloned.1.call-update) | async-done | bytes 153616 | tf_op jit(solution)/shard_map/reduce_scatter | solution.py:17
  306.5 1.7 copy.8
  308.2 4.8 %all-to-all-start = ((f32[32,1,1200]{2,1,0:T(1,128)}), f32[32,1,1200]{2,1,0:T(1,128)S(1)}, u32[]{:S(2)}, u32[]{:S(2)}) async-start(f32[32,1,1200]{2,1,0:T(1,128)} %copy.8), calls=%async_computation.1 | async-start | bytes 327680 | tf_op jit(solution)/shard_map/all_to_all | solution.py:26
  313.1 0.0 copy-done.1
  313.1 0.0 copy-done.2
  313.1 0.1 broadcast_subtract_fusion
  313.2 6.7 %all-to-all-done = f32[32,1,1200]{2,1,0:T(1,128)S(1)} async-done(((f32[32,1,1200]{2,1,0:T(1,128)}), f32[32,1,1200]{2,1,0:T(1,128)S(1)}, u32[]{:S(2)}, u32[]{:S(2)}) %all-to-all-start) | async-done | bytes 153632 | tf_op jit(solution)/shard_map/all_to_all | solution.py:26
  319.8 0.0 copy-done
  319.8 0.8 bitcast_divide_fusion
Async XLA Ops:
  6.5 119.5 %all-gather.2.cloned.1.call-start = ((), (), s32[]{:S(2)}) async-start(), calls=%async_computation.2 | async-start | bytes 11059200 | tf_op jit(solution)/shard_map/all_gather | solution.py:9
  7.3 299.2 %reduce-scatter.2.cloned.1.call-start = ((), (), s32[]{:S(2)}) async-start(), calls=%async_computation.3 | async-start | bytes 5406720 | tf_op jit(solution)/shard_map/reduce_scatter | solution.py:17
  126.1 187.0 %copy-start.1 = (f32[8]{0:T(128)S(1)}, f32[8]{0:T(128)}, u32[]{:S(2)}) copy-start(f32[8]{0:T(128)} %param.8) | copy-start | bytes 100
  126.1 187.0 %copy-start.2 = (f32[4]{0:T(128)S(1)}, f32[4]{0:T(128)}, u32[]{:S(2)}) copy-start(f32[4]{0:T(128)} %param.7) | copy-start | bytes 52
  126.1 193.7 %copy-start = (f32[1200]{0:T(1024)S(1)}, f32[1200]{0:T(1024)}, u32[]{:S(2)}) copy-start(f32[1200]{0:T(1024)} %param.9) | copy-start | bytes 14404
  308.2 11.6 %all-to-all-start = ((f32[32,1,1200]{2,1,0:T(1,128)}), f32[32,1,1200]{2,1,0:T(1,128)S(1)}, u32[]{:S(2)}, u32[]{:S(2)}) async-start(f32[32,1,1200]{2,1,0:T(1,128)} %copy.8), calls=%async_computation.1 | async-start | bytes 327680 | tf_op jit(solution)/shard_map/all_to_all | solution.py:26
Sparse Core Ops, SparseCore 0:
  9.1 116.9 all-gather.1
  173.8 132.6 reduce-scatter.1
where the time goes:
time: 328 us; the launch traced here: 327 us
  waiting for transfers between devices  249 us (76%)
  matrix products  47.6 us (15%)
  between operations  13.4 us (4%)
  local copies, waits for them, and re-layouts  11.5 us (4%)
  starting transfers between devices  4.87 us (1%)
    reduce_scatter x1, waiting for transfers between devices, per_device(): lax.psum_scatter(jnp.dot(flattened, weights, precision=lax.Precision.HIGH...  133 us
    all_gather x1, waiting for transfers between devices, per_device(): gathered = lax.all_gather(amplitudes, 'col', axis=0, tiled=True)  109 us
    dot_general x1, matrix products, per_device(): jnp.dot(flattened, weights, precision=lax.Precision.HIGHEST, preferred_el...  47.6 us
    unnamed x7, local copies, waits for them, and re-layouts  9.78 us
    all_to_all x1, waiting for transfers between devices, per_device(): lax.all_to_all(reshaped, 'col', split_axis=0, concat_axis=1, tiled=True)  6.67 us
  transfers between devices with their start and end apart: 3, of which 3 were waited for; matrix products, arithmetic and copies ran while one was open for 3% of the time, Pallas kernels for 0%

commit v1 on v0

--- a/solution.py
+++ b/solution.py
@@ -2,6 +2,19 @@
 import jax.numpy as jnp
 from jax import lax
 from jax.sharding import PartitionSpec as P
+
+
+def halves_turn(x0):
+    front = jnp.concatenate(
+        lax.all_to_all(
+            jnp.stack(jnp.split(x0, lax.axis_size("col"), axis=0), axis=0),
+            "col",
+            concat_axis=0,
+            split_axis=0,
+        ),
+        axis=1,
+    )
+    return front
 
 
 def per_device(amplitudes, integrals, pair_energy, block_energy, virtual_energy):
@@ -23,7 +36,7 @@
         tiled=True,
     )
     reshaped = summed.reshape(row_block, a_local, virt_width)
-    arrived = lax.all_to_all(reshaped, "col", split_axis=0, concat_axis=1, tiled=True)
+    arrived = halves_turn(reshaped)
     denominator = (
         pair_energy[:, None, None] - block_energy[None, :, None] - virtual_energy[None, None, :]
     )

time: 328 us -> 338 us (1.030)
  local copies, waits for them, and re-layouts: 11.5 us -> 21.6 us
    unnamed x7 -> x14, local copies, waits for them, and re-layouts: 9.78 us -> 19.5 us
where the time goes in v1:
time: 338 us; the launch traced here: 337 us
  waiting for transfers between devices  249 us (74%)
  matrix products  47.6 us (14%)
  local copies, waits for them, and re-layouts  21.6 us (6%)
  between operations  13.4 us (4%)
  starting transfers between devices  4.87 us (1%)
    reduce_scatter x1, waiting for transfers between devices, per_device(): lax.psum_scatter(jnp.dot(flattened, weights, precision=lax.Precision.HIGH...  133 us
    all_gather x1, waiting for transfers between devices, per_device(): gathered = lax.all_gather(amplitudes, 'col', axis=0, tiled=True)  109 us
    dot_general x1, matrix products, per_device(): jnp.dot(flattened, weights, precision=lax.Precision.HIGHEST, preferred_el...  47.6 us
    unnamed x14, local copies, waits for them, and re-layouts  19.5 us
  transfers between devices with their start and end apart: 3, of which 3 were waited for; matrix products, arithmetic and copies ran while one was open for 3% of the time, Pallas kernels for 0%

profile of v1, /device:TPU:4, one launch (start us, length us, event | category | flops | bytes accessed | tf_op | source)
XLA Modules:
  0.0 336.8 jit_solution(9526004845052984429)
XLA Ops:
  6.5 0.0 all-gather.2.cloned.1.call-start
  6.5 0.7 all-gather.2.cloned.1.call-update
  7.3 0.0 reduce-scatter.2.cloned.1.call-start
  7.3 9.8 %copy.8 = f32[2,1200,1,1200]{3,1,2,0:T(8,128)} copy(f32[2,1200,1,1200]{3,2,1,0:T(1,128)} %param.6) | data formatting | bytes 23040000
  17.1 109.0 %all-gather.2.cloned.1.call-done = f32[1024,2,1200]{0,2,1:T(8,128)} async-done(((f32[128,2,1200]{0,2,1:T(8,128)}), f32[1024,2,1200]{0,2,1:T(8,128)}) %all-gather.2.cloned.1.call-update) | async-done | bytes 9830416 | tf_op jit(solution)/shard_map/all_gather | solution.py:22
  126.1 0.0 copy-start.1
  126.1 0.0 copy-start.2
  126.1 0.0 copy-start
  126.1 47.6 %fusion.8 = f32[1024,1200]{1,0:T(8,128)} fusion(f32[1024,2400]{0,1:T(8,128)} %bitcast.41, f32[2400,1200]{1,0:T(8,128)} %bitcast.40), kind=kOutput, calls=%fused_computation.18 | convolution fusion | flops 35389440000 | bytes 26265600 | tf_op jit(solution)/shard_map/dot_general | solution.py:31
  173.7 0.0 reduce-scatter.2.cloned.1.call-update
  173.7 132.8 %reduce-scatter.2.cloned.1.call-done = f32[32,1200]{1,0:T(8,128)} async-done(((f32[1024,1200]{1,0:T(8,128)}), f32[32,1200]{1,0:T(8,128)}) %reduce-scatter.2.cloned.1.call-update) | async-done | bytes 153616 | tf_op jit(solution)/shard_map/reduce_scatter | solution.py:30
  306.5 1.4 fusion.7
  307.9 1.4 fusion.6
  309.3 1.4 fusion.5
  310.7 1.4 fusion.4
  312.0 1.4 fusion.3
  313.4 1.4 fusion.2
  314.8 1.4 fusion.1
  316.2 1.4 fusion
  317.6 4.8 %all-to-all-start = ((f32[8,4,1,1200]{3,1,2,0:T(4,128)}), f32[8,4,1,1200]{3,1,2,0:T(4,128)S(1)}, u32[]{:S(2)}, u32[]{:S(2)}) async-start(f32[8,4,1,1200]{3,1,2,0:T(4,128)} %fusion), calls=%async_computation.1 | async-start | bytes 327680 | tf_op jit(solution)/shard_map/all_to_all | solution.py:9
  322.4 0.0 copy-done.1
  322.4 0.0 copy-done.2
  322.4 0.1 broadcast_subtract_fusion
  322.5 6.7 %all-to-all-done = f32[8,4,1,1200]{3,1,2,0:T(4,128)S(1)} async-done(((f32[8,4,1,1200]{3,1,2,0:T(4,128)}), f32[8,4,1,1200]{3,1,2,0:T(4,128)S(1)}, u32[]{:S(2)}, u32[]{:S(2)}) %all-to-all-start) | async-done | bytes 153632 | tf_op jit(solution)/shard_map/all_to_all | solution.py:9
  329.2 0.0 copy-done
  329.2 0.1 bitcast_divide_fusion
  329.3 0.7 copy.7
Async XLA Ops:
  6.5 119.5 %all-gather.2.cloned.1.call-start = ((), (), s32[]{:S(2)}) async-start(), calls=%async_computation.2 | async-start | bytes 11059200 | tf_op jit(solution)/shard_map/all_gather | solution.py:22
  7.3 299.2 %reduce-scatter.2.cloned.1.call-start = ((), (), s32[]{:S(2)}) async-start(), calls=%async_computation.3 | async-start | bytes 5406720 | tf_op jit(solution)/shard_map/reduce_scatter | solution.py:30
  126.1 196.4 %copy-start.1 = (f32[8]{0:T(128)S(1)}, f32[8]{0:T(128)}, u32[]{:S(2)}) copy-start(f32[8]{0:T(128)} %param.8) | copy-start | bytes 100
  126.1 196.4 %copy-start.2 = (f32[4]{0:T(128)S(1)}, f32[4]{0:T(128)}, u32[]{:S(2)}) copy-start(f32[4]{0:T(128)} %param.7) | copy-start | bytes 52
  126.1 203.1 %copy-start = (f32[1200]{0:T(1024)S(1)}, f32[1200]{0:T(1024)}, u32[]{:S(2)}) copy-start(f32[1200]{0:T(1024)} %param.9) | copy-start | bytes 14404
  317.6 11.6 %all-to-all-start = ((f32[8,4,1,1200]{3,1,2,0:T(4,128)}), f32[8,4,1,1200]{3,1,2,0:T(4,128)S(1)}, u32[]{:S(2)}, u32[]{:S(2)}) async-start(f32[8,4,1,1200]{3,1,2,0:T(4,128)} %fusion), calls=%async_computation.1 | async-start | bytes 327680 | tf_op jit(solution)/shard_map/all_to_all | solution.py:9
Sparse Core Ops, SparseCore 0:
  9.1 116.9 all-gather.1
  173.8 132.6 reduce-scatter.1

commit v2 on v0

--- a/solution.py
+++ b/solution.py
@@ -6,7 +6,9 @@
 
 def per_device(amplitudes, integrals, pair_energy, block_energy, virtual_energy):
     row_size = lax.axis_size("row")
-    gathered = lax.all_gather(amplitudes, "col", axis=0, tiled=True)
+    gathered = jnp.concatenate(
+        lax.all_to_all(jnp.stack([amplitudes] * lax.psum(1, "col")), "col", 0, 0), axis=0
+    )
     pair_count = gathered.shape[0]
     contract_len = gathered.shape[1] * gathered.shape[2]
     flattened = gathered.reshape(pair_count, contract_len)

time: 328 us -> 372 us (1.13)
  matrix products: 47.6 us -> 82.1 us
  local copies, waits for them, and re-layouts: 11.5 us -> 26.8 us
  waiting for transfers between devices: 249 us -> 239 us
  starting transfers between devices: 4.87 us -> 9.93 us
    all_gather x1 -> x0, waiting for transfers between devices: 109 us -> none  [per_device(): gathered = lax.all_gather(amplitudes, 'col', axis=0, tiled=True)]
    all_to_all x0 -> x1, waiting for transfers between devices: none -> 99.4 us  [per_device(): lax.all_to_all(jnp.stack([amplitudes] * lax.psum(1, 'col')), 'col', 0, 0)]
    dot_general x1, matrix products: 47.6 us -> 82.1 us  [per_device(): jnp.dot(flattened, weights, precision=lax.Precision.HIGHEST, preferred_el...]
    all_to_all x0 -> x1, local copies, waits for them, and re-layouts: none -> 9.54 us  [per_device(): lax.all_to_all(jnp.stack([amplitudes] * lax.psum(1, 'col')), 'col', 0, 0)]
    another operation x0 -> x1, local copies, waits for them, and re-layouts: none -> 5.68 us  [per_device(): jnp.stack([amplitudes] * lax.psum(1, 'col'))]
    all_to_all x0 -> x1, starting transfers between devices: none -> 5.15 us  [per_device(): lax.all_to_all(jnp.stack([amplitudes] * lax.psum(1, 'col')), 'col', 0, 0)]
    unnamed x7 -> x9, local copies, waits for them, and re-layouts: 9.78 us -> 9.79 us
where the time goes in v2:
time: 372 us
  waiting for transfers between devices  239 us (64%)
  matrix products  82.1 us (22%)
  local copies, waits for them, and re-layouts  26.8 us (7%)
  between operations  13.5 us (4%)
  starting transfers between devices  9.93 us (3%)
    reduce_scatter x1, waiting for transfers between devices, per_device(): lax.psum_scatter(jnp.dot(flattened, weights, precision=lax.Precision.HIGH...  133 us
    all_to_all x1, waiting for transfers between devices, per_device(): lax.all_to_all(jnp.stack([amplitudes] * lax.psum(1, 'col')), 'col', 0, 0)  99.4 us
    dot_general x1, matrix products, per_device(): jnp.dot(flattened, weights, precision=lax.Precision.HIGHEST, preferred_el...  82.1 us
    unnamed x9, local copies, waits for them, and re-layouts  9.79 us
    all_to_all x1, local copies, waits for them, and re-layouts, per_device(): lax.all_to_all(jnp.stack([amplitudes] * lax.psum(1, 'col')), 'col', 0, 0)  9.54 us
  transfers between devices with their start and end apart: 3, of which 3 were waited for; matrix products, arithmetic and copies ran while one was open for 3% of the time, Pallas kernels for 0%

profile of v2, /device:TPU:4, one launch (start us, length us, event | category | flops | bytes accessed | tf_op | source)
XLA Modules:
  0.0 372.1 jit_solution(11598209096059715557)
XLA Ops:
  6.5 5.7 %stack.2 = f32[8,128,2,1200]{1,3,2,0:T(8,128)} broadcast(f32[128,2,1200]{0,2,1:T(8,128)} %param.5), dimensions={1,2,3} | broadcast | bytes 11059200 | tf_op jit(solution)/shard_map/stack | solution.py:10
  12.2 5.1 %all-to-all-start = ((f32[8,128,2,1200]{1,3,2,0:T(8,128)}), f32[8,128,2,1200]{1,3,2,0:T(8,128)}, u32[]{:S(2)}, u32[]{:S(2)}) async-start(f32[8,128,2,1200]{1,3,2,0:T(8,128)} %stack.2), calls=%async_computation | async-start | bytes 19660800 | tf_op jit(solution)/shard_map/all_to_all | solution.py:10
  17.4 0.0 reduce-scatter.2.cloned.1.call-start
  17.4 9.8 %copy.12 = f32[2,1200,1,1200]{3,1,2,0:T(8,128)} copy(f32[2,1200,1,1200]{3,2,1,0:T(1,128)} %param.6) | data formatting | bytes 23040000
  27.2 99.4 %all-to-all-done = f32[8,128,2,1200]{1,3,2,0:T(8,128)} async-done(((f32[8,128,2,1200]{1,3,2,0:T(8,128)}), f32[8,128,2,1200]{1,3,2,0:T(8,128)}, u32[]{:S(2)}, u32[]{:S(2)}) %all-to-all-start) | async-done | bytes 9830432 | tf_op jit(solution)/shard_map/all_to_all | solution.py:10
  126.6 0.0 copy-start
  126.6 9.5 %copy.9 = f32[8,128,2,1200]{1,0,3,2:T(8,128)S(1)} copy(f32[8,128,2,1200]{1,3,2,0:T(8,128)} %all-to-all-done) | data formatting | bytes 19660800 | tf_op jit(solution)/shard_map/all_to_all | solution.py:10
  136.1 0.0 copy-done
  136.1 0.0 copy-start.2
  136.1 0.0 copy-start.3
  136.1 0.0 copy-start.1
  136.2 82.1 %fusion = f32[1024,1200]{1,0:T(8,128)} fusion(f32[2400,1200]{1,0:T(8,128)S(1)} %bitcast.15, f32[300,8,8,128]{3,2,1,0:T(8,128)S(1)} %bitcast.16), kind=kOutput, calls=%fused_computation | convolution fusion | flops 35389440000 | bytes 26265600 | tf_op jit(solution)/shard_map/dot_general | solution.py:20
  218.2 0.0 reduce-scatter.2.cloned.1.call-update
  218.3 133.0 %reduce-scatter.2.cloned.1.call-done = f32[32,1200]{1,0:T(8,128)} async-done(((f32[1024,1200]{1,0:T(8,128)}), f32[32,1200]{1,0:T(8,128)}) %reduce-scatter.2.cloned.1.call-update) | async-done | bytes 153616 | tf_op jit(solution)/shard_map/reduce_scatter | solution.py:19
  351.3 1.7 copy.10
  353.0 4.7 %all-to-all-start.1 = ((f32[32,1,1200]{2,1,0:T(1,128)}), f32[32,1,1200]{2,1,0:T(1,128)S(1)}, u32[]{:S(2)}, u32[]{:S(2)}) async-start(f32[32,1,1200]{2,1,0:T(1,128)} %copy.10), calls=%async_computation.2 | async-start | bytes 327680 | tf_op jit(solution)/shard_map/all_to_all | solution.py:28
  357.8 0.0 copy-done.2
  357.8 0.0 copy-done.3
  357.8 0.1 broadcast_subtract_fusion
  357.9 6.7 %all-to-all-done.1 = f32[32,1,1200]{2,1,0:T(1,128)S(1)} async-done(((f32[32,1,1200]{2,1,0:T(1,128)}), f32[32,1,1200]{2,1,0:T(1,128)S(1)}, u32[]{:S(2)}, u32[]{:S(2)}) %all-to-all-start.1) | async-done | bytes 153632 | tf_op jit(solution)/shard_map/all_to_all | solution.py:28
  364.5 0.0 copy-done.1
  364.5 0.8 bitcast_divide_fusion
Async XLA Ops:
  12.2 114.3 %all-to-all-start = ((f32[8,128,2,1200]{1,3,2,0:T(8,128)}), f32[8,128,2,1200]{1,3,2,0:T(8,128)}, u32[]{:S(2)}, u32[]{:S(2)}) async-start(f32[8,128,2,1200]{1,3,2,0:T(8,128)} %stack.2), calls=%async_computation | async-start | bytes 19660800 | tf_op jit(solution)/shard_map/all_to_all | solution.py:10
  17.4 333.9 %reduce-scatter.2.cloned.1.call-start = ((), (), s32[]{:S(2)}) async-start(), calls=%async_computation.3 | async-start | bytes 5406720 | tf_op jit(solution)/shard_map/reduce_scatter | solution.py:19
  126.6 9.6 %copy-start = (f32[2,1200,1,1200]{3,1,2,0:T(8,128)S(1)}, f32[2,1200,1,1200]{3,1,2,0:T(8,128)}, u32[]{:S(2)}) copy-start(f32[2,1200,1,1200]{3,1,2,0:T(8,128)} %copy.12) | copy-start | bytes 34560004
  136.1 221.6 %copy-start.2 = (f32[8]{0:T(128)S(1)}, f32[8]{0:T(128)}, u32[]{:S(2)}) copy-start(f32[8]{0:T(128)} %param.8) | copy-start | bytes 100
  136.1 221.6 %copy-start.3 = (f32[4]{0:T(128)S(1)}, f32[4]{0:T(128)}, u32[]{:S(2)}) copy-start(f32[4]{0:T(128)} %param.7) | copy-start | bytes 52
  136.1 228.4 %copy-start.1 = (f32[1200]{0:T(1024)S(1)}, f32[1200]{0:T(1024)}, u32[]{:S(2)}) copy-start(f32[1200]{0:T(1024)} %param.9) | copy-start | bytes 14404
  353.0 11.5 %all-to-all-start.1 = ((f32[32,1,1200]{2,1,0:T(1,128)}), f32[32,1,1200]{2,1,0:T(1,128)S(1)}, u32[]{:S(2)}, u32[]{:S(2)}) async-start(f32[32,1,1200]{2,1,0:T(1,128)} %copy.10), calls=%async_computation.2 | async-start | bytes 327680 | tf_op jit(solution)/shard_map/all_to_all | solution.py:28
Sparse Core Ops, SparseCore 0:
  218.4 132.8 reduce-scatter.1
